TPU v7x, 512 devices: a whole 4x8x8 slice. The times are simulated.
512 devices in a mesh: pb: 16 (over y, core), ka: 32 (over x, z).
Axes of the slice: x: 4, y: 8, z: 8, core: 2. Of those that a mesh axis runs over, the one named last changes fastest.
Arguments:
- coupling: bfloat16 [16, 1728, 2, 1600], P('pb', 'ka'), may hold values from -6 to 6
- rot_k: bfloat16 [1728, 2, 1600], P('ka'), may hold values from -0.625 to 0.625
- rot_kq: bfloat16 [16, 1728, 2, 1600], P('pb', 'ka'), may hold values from -0.625 to 0.625
- r_elec: int32 [2048, 3], replicated, may hold values from -6 to 6
- degen: int32 [2048], replicated, may hold values from 1 to 8
- reader: int32 [2048, 1], replicated, may hold values from 0 to 31; in each aligned block of 2048 rows (0 to 2047, 2048 to 4095, ...) at most 128 rows name the same one
- r_phon: int32 [32, 3], replicated, may hold values from -3 to 3
Outputs:
- wannier: float32 [32, 2, 1600, 4096], P(None, None, 'pb', 'ka')
Inputs may be any that keep to these rules, and one draw needn't show every extreme that they name: Each reader is named by at most 128 lattice vectors, and one reader by exactly 128.
All inputs are finite; a program needn't handle non-finite values.
Results may differ from a plain program's by a relative error of at most 0.0056.
Values may be sent and summed in bfloat16 or wider, within the bound.
A program may use at most 128 MiB of HBM per device.

v0:
```python
import math
import jax
import jax.numpy as jnp
from jax import lax
from jax.sharding import PartitionSpec as P

W = 40
KGRID = 12
QGRID = 6


def angle_tables(vectors, count, grid):
    index = jnp.arange(count, dtype=jnp.int32)
    first = index // (grid * grid)
    second = index // grid % grid
    third = index % grid
    inner = (
        vectors[:, 0:1] * first[None, :]
        + vectors[:, 1:2] * second[None, :]
        + vectors[:, 2:3] * third[None, :]
    )
    angle = jnp.mod(inner, grid).astype(jnp.float32) * (2.0 * math.pi / grid)
    return (jnp.cos(angle).astype(jnp.bfloat16), jnp.sin(angle).astype(jnp.bfloat16))


def slot_tables(reader, degen, readers, most):
    reader_row = reader[:, 0]
    member = (reader_row[:, None] == jnp.arange(readers, dtype=jnp.int32)[None, :]).astype(
        jnp.int32
    )
    ranking = jnp.sum((jnp.cumsum(member, axis=0) - 1) * member, axis=1)
    position = reader_row * most + ranking
    source_row = (
        jnp.full((readers * most,), -1, jnp.int32)
        .at[position]
        .set(jnp.arange(reader_row.shape[0], dtype=jnp.int32))
    )
    usable = source_row >= 0
    source_row = jnp.maximum(source_row, 0)
    inverse_deg = jnp.where(usable, 1.0 / degen[source_row].astype(jnp.float32), jnp.float32(0.0))
    return (position, source_row, usable, inverse_deg)


def product(spec, left, right):
    return jnp.einsum(spec, left, right, preferred_element_type=jnp.float32)


def rotate(coupling, rot_k, rot_kq):
    q_local, k_local = (coupling.shape[0], coupling.shape[1])
    g_mat = coupling.reshape(q_local, k_local, 2, W, W)
    u_mat = rot_k.reshape(k_local, 2, W, W)
    v_mat = rot_kq.reshape(q_local, k_local, 2, W, W)
    spec = "qkab,kbn->qkan"
    x_real = product(spec, g_mat[:, :, 0], u_mat[:, 0]) - product(spec, g_mat[:, :, 1], u_mat[:, 1])
    x_imag = product(spec, g_mat[:, :, 0], u_mat[:, 1]) + product(spec, g_mat[:, :, 1], u_mat[:, 0])
    x_real = x_real.astype(jnp.bfloat16)
    x_imag = x_imag.astype(jnp.bfloat16)
    spec_two = "qkam,qkan->qkmn"
    y_real = product(spec_two, v_mat[:, :, 0], x_real) + product(spec_two, v_mat[:, :, 1], x_imag)
    y_imag = product(spec_two, v_mat[:, :, 0], x_imag) - product(spec_two, v_mat[:, :, 1], x_real)
    return jnp.stack([y_real, y_imag], 2).reshape(q_local, k_local, 2, W * W).astype(jnp.bfloat16)


def per_device(coupling, rot_k, rot_kq, r_elec, degen, reader, r_phon):
    ka_count = lax.axis_size("ka")
    pb_count = lax.axis_size("pb")
    q_local, k_local, width_sq = (coupling.shape[0], coupling.shape[1], coupling.shape[3])
    total_k = k_local * ka_count
    total_r = r_elec.shape[0]
    most = 2 * total_r // ka_count
    scale = total_k ** (-0.5)
    rotated = rotate(coupling, rot_k, rot_kq)
    position, source_row, usable, inverse_deg = slot_tables(reader, degen, ka_count, most)
    offset = lax.axis_index("ka") * most
    my_rows = lax.dynamic_slice_in_dim(source_row, offset, most)
    my_usable = lax.dynamic_slice_in_dim(usable, offset, most)
    my_vectors = r_elec[my_rows]
    keep = my_usable.astype(jnp.bfloat16)[:, None]
    span = q_local * width_sq
    piece = lax.all_gather(rotated, "ka", axis=1, tiled=True)
    count = piece.shape[1]
    cosine, sine = angle_tables(my_vectors, count, KGRID)
    left = jnp.concatenate([cosine * keep, sine * keep], axis=1)
    z_real = piece[:, :, 0].transpose(1, 0, 2).reshape(count, span)
    z_imag = piece[:, :, 1].transpose(1, 0, 2).reshape(count, span)
    upper = jnp.concatenate([z_real, z_imag], axis=1)
    lower = jnp.concatenate([z_imag, -z_real], axis=1)
    right = jnp.concatenate([upper, lower], axis=0)
    summed = jnp.dot(left, right, preferred_element_type=jnp.float32)
    real_sum = summed[:, :span]
    imag_sum = summed[:, span:]
    stacked = jnp.stack(
        [real_sum.reshape(most, q_local, width_sq), imag_sum.reshape(most, q_local, width_sq)], 2
    )
    mine = (stacked * scale).astype(jnp.bfloat16)
    gathered_q = lax.all_to_all(mine, "pb", split_axis=3, concat_axis=1, tiled=True)
    total_q = q_local * pb_count
    slim = gathered_q.shape[3]
    phonon_count = r_phon.shape[0]
    q_cos, q_sin = angle_tables(r_phon, total_q, QGRID)
    flat = gathered_q.transpose(1, 0, 2, 3).reshape(total_q, most * 2 * slim)
    c_part = jnp.dot(q_cos, flat, preferred_element_type=jnp.float32).reshape(
        phonon_count, most, 2, slim
    )
    s_part = jnp.dot(q_sin, flat, preferred_element_type=jnp.float32).reshape(
        phonon_count, most, 2, slim
    )
    real_out = c_part[:, :, 0] + s_part[:, :, 1]
    imag_out = c_part[:, :, 1] - s_part[:, :, 0]
    result = jnp.stack([real_out, imag_out], 1).transpose(0, 1, 3, 2)
    my_inverse = lax.dynamic_slice_in_dim(inverse_deg, offset, most)
    return result * (my_inverse * total_q ** (-0.5))[None, None, None, :]


def solution(mesh):
    in_specs = (
        P("pb", "ka", None, None),
        P("ka", None, None),
        P("pb", "ka", None, None),
        P(),
        P(),
        P(),
        P(),
    )
    out_specs = P(None, None, "pb", "ka")
    return jax.shard_map(
        per_device, mesh=mesh, in_specs=in_specs, out_specs=out_specs, check_vma=False
    )
```

profile of v0, /device:TPU:1, one launch (start us, length us, event | category | flops | bytes accessed | tf_op | source)
XLA Modules:
  0.0 320.0 jit_solution(17944751337558424967)
XLA Ops:
  6.5 1.1 copy.55
  7.6 1.0 reshape.274
  8.7 1.7 reshape.311
  10.8 1.5 fusion.29
  12.3 1.3 fusion.19
  14.4 2.0 reshape.278
  16.4 1.8 fusion.18
  19.6 1.0 copy.58
  20.7 1.5 stack.21
  24.6 9.1 %reduce-window.6 = s32[32,16,128]{2,1,0:T(8,128)S(1)} reduce-window(s32[32,16,128]{2,1,0:T(8,128)S(1)} %fusion.36, s32[]{:T(128)} %constant.88.clone.1), window={size=1x1x128 pad=0_0x0_0x127_0}, to_apply=%region_0.0 | reduce-window | flops 8323072 | bytes 524292 | tf_op jit(solution)/shard_map/reduce-window
  34.9 8.2 %scatter_custom_fusion = s32[4096]{0:T(1024)S(1)} fusion(s32[2048]{0:T(1024)S(1)} %bitcast.125, s32[2048]{0:T(1024)S(1)} %iota.45, s32[]{:T(128)} %constant.90.clone.1), kind=kCustom, calls=%fused_computation.94 | custom fusion | bytes 16388 | tf_op jit(solution)/shard_map/scatter | solution.py:36
  44.2 4.3 %fusion.32 = (bf16[128,1728]{1,0:T(8,128)(2,1)S(1)}, bf16[128,1728]{1,0:T(8,128)(2,1)S(1)}) fusion(s32[1728]{0:T(1024)S(1)} %get-tuple-element.21, s32[128]{0:T(128)S(1)} %get-tuple-element.7, s32[1728]{0:T(1024)S(1)} %get-tuple-element.22, s32[128]{0:T(128)S(1)} %get-tuple-element.6, s32[1728]{0:T(1024)S(1)} %add_select_fusion.4, ...), kind=kLoop, calls=%fused_computation.56 | loop fusion | flops 4866048 | bytes 907264 | tf_op jit(solution)/shard_map/mul | solution.py:83
  48.5 100.7 %all-gather.2.cloned.1.call-done = bf16[1,1728,2,1600]{3,2,0,1:T(2,128)(2,1)} async-done(((bf16[1,54,2,1600]{3,2,0,1:T(2,128)(2,1)}), bf16[1,1728,2,1600]{3,2,0,1:T(2,128)(2,1)}) %all-gather.2.cloned.1.call-update) | async-done | bytes 11059216 | tf_op jit(solution)/shard_map/all_gather | solution.py:80
  149.2 23.0 %fusion.69 = (bf16[1,1728,1,1600]{3,2,0,1:T(2,128)(2,1)}, bf16[1,1728,1,1600]{3,2,0,1:T(2,128)(2,1)}) fusion(bf16[1,1728,2,1600]{3,2,0,1:T(2,128)(2,1)} %all-gather.2.cloned.1.call-done), kind=kLoop, calls=%fused_computation.131 | loop fusion | bytes 22118400 | tf_op jit(solution)/shard_map/slice | solution.py:85
  172.2 25.3 %copy.80 = bf16[1,1728,1,1600]{1,3,2,0:T(8,128)(2,1)} copy(bf16[1,1728,1,1600]{3,2,0,1:T(2,128)(2,1)} %get-tuple-element.9) | data formatting | bytes 11059200
  197.5 5.4 %bitcast_negate_fusion = bf16[1728,1600]{0,1:T(8,128)(2,1)} fusion(bf16[1,1728,1,1600]{1,3,2,0:T(8,128)(2,1)} %copy.80), kind=kLoop, calls=%fused_computation.124 | loop fusion | flops 2764800 | bytes 11059200 | tf_op jit(solution)/shard_map/neg | solution.py:87
  202.9 25.2 %copy.81 = bf16[1,1728,1,1600]{1,3,2,0:T(8,128)(2,1)} copy(bf16[1,1728,1,1600]{3,2,0,1:T(2,128)(2,1)} %get-tuple-element.8) | data formatting | bytes 11059200
  228.1 30.9 %fusion = f32[128,3200]{0,1:T(8,128)S(1)} fusion(bf16[1728,1600]{0,1:T(8,128)(2,1)} %bitcast_negate_fusion, bf16[1728,1600]{0,1:T(8,128)(2,1)} %bitcast.115, bf16[1728,1600]{0,1:T(8,128)(2,1)} %bitcast.114, bf16[128,1728]{1,0:T(8,128)(2,1)S(1)} %get-tuple-element.15, bf16[128,1728]{1,0:T(8,128)(2,1)S(1)} %get-tuple-element.14), kind=kOutput, calls=%fused_computation.3 | convolution fusion | flops 2921398272 | bytes 19111936 | tf_op jit(solution)/shard_map/dot_general | solution.py:89
  259.3 7.8 %copy.65 = bf16[128,1,2,1600]{0,2,1,3:T(2,128)(2,1)} copy(bf16[128,1,2,1600]{0,3,2,1:T(8,128)(2,1)S(1)} %fusion.11) | data formatting | bytes 1638400 | tf_op jit(solution)/shard_map/convert_element_type | solution.py:95
  267.0 8.0 %all-to-all-start = ((bf16[128,1,2,1600]{0,2,1,3:T(2,128)(2,1)}), bf16[128,1,2,1600]{0,2,1,3:T(2,128)(2,1)S(1)}, u32[]{:S(2)}, u32[]{:S(2)}) async-start(bf16[128,1,2,1600]{0,2,1,3:T(2,128)(2,1)} %copy.65), calls=%async_computation | async-start | bytes 1638400 | tf_op jit(solution)/shard_map/all_to_all | solution.py:96
  275.0 23.0 %gather_fusion.1 = s32[4096]{0:T(1024)S(1)} fusion(s32[2048]{0:T(1024)S(1)} %copy-done, s32[4096]{0:T(1024)S(1)} %get-tuple-element.16), kind=kCustom, calls=%fused_computation.1 | custom fusion | bytes 49152 | tf_op jit(solution)/shard_map/gather | solution.py:40
  299.4 2.0 reshape.282
  301.4 4.0 %dot_general.47 = bf16[128,2,100,16]{2,1,0,3:T(2,128)(2,1)S(1)} reshape(bf16[25600,16]{0,1:T(8,128)(2,1)S(1)} %bitcast.117) | data formatting | bytes 1638400 | tf_op jit(solution)/shard_map/dot_general | solution.py:102
  308.9 4.2 %copy.70 = f32[32,2,100,128]{3,1,2,0:T(2,128)} copy(f32[32,2,100,128]{3,0,2,1:T(8,128)S(1)} %fusion.8) | data formatting | bytes 6553600 | tf_op jit(solution)/shard_map/mul | solution.py:112
  (60 shorter events, 12.2 us)
Async XLA Ops:
  6.5 268.5 %copy-start = (s32[2048]{0:T(1024)S(1)}, s32[2048]{0:T(1024)}, u32[]{:S(2)}) copy-start(s32[2048]{0:T(1024)} %param.11) | copy-start | bytes 24580
  6.5 2.1 copy-start.3
  6.5 142.7 %all-gather.2.cloned.1.call-start = ((), (), s32[]{:S(2)}) async-start(), calls=%async_computation.1 | async-start | bytes 11860992 | tf_op jit(solution)/shard_map/all_gather | solution.py:80
  12.3 1.3 copy-start.4
  16.4 1.8 copy-start.1
  19.2 3.1 copy-start.2
  22.7 1.9 copy-start.5
  23.4 10.8 %copy-start.6 = (s32[2048,3]{0,1:T(4,128)S(1)}, s32[2048,3]{0,1:T(4,128)}, u32[]{:S(2)}) copy-start(s32[2048,3]{0,1:T(4,128)} %param.10) | copy-start | bytes 73732
  267.0 31.4 %all-to-all-start = ((bf16[128,1,2,1600]{0,2,1,3:T(2,128)(2,1)}), bf16[128,1,2,1600]{0,2,1,3:T(2,128)(2,1)S(1)}, u32[]{:S(2)}, u32[]{:S(2)}) async-start(bf16[128,1,2,1600]{0,2,1,3:T(2,128)(2,1)} %copy.65), calls=%async_computation | async-start | bytes 1638400 | tf_op jit(solution)/shard_map/all_to_all | solution.py:96
  275.0 23.2 %copy-start.7 = (s32[32,3]{0,1:T(4,128)S(1)}, s32[32,3]{0,1:T(4,128)}, u32[]{:S(2)}) copy-start(s32[32,3]{0,1:T(4,128)} %param.13) | copy-start | bytes 1156
Sparse Core Ops, SparseCore 0:
  24.7 124.4 all-gather.1
where the time goes:
time: 322 us; the launch traced here: 320 us
  local copies, waits for them, and re-layouts  137 us (43%)
  waiting for transfers between devices  101 us (31%)
  matrix products  39.3 us (12%)
  other arithmetic  21 us (7%)
  between operations  13.8 us (4%)
  starting transfers between devices  7.98 us (2%)
    all_gather x1, waiting for transfers between devices, per_device(): piece = lax.all_gather(rotated, 'ka', axis=1, tiled=True)  101 us
    unnamed x21, local copies, waits for them, and re-layouts  52.7 us
    dot_general x1, matrix products, per_device(): summed = jnp.dot(left, right, preferred_element_type=jnp.float32)  30.9 us
    gather x1, local copies, waits for them, and re-layouts, slot_tables(): degen[source_row].astype(jnp.float32)  23 us
    slice x1, local copies, waits for them, and re-layouts, per_device(): z_imag = piece[:, :, 1].transpose(1, 0, 2).reshape(count, span)  23 us
    another operation x2, other arithmetic  9.27 us
    scatter x1, local copies, waits for them, and re-layouts, slot_tables(): source_row = jnp.full((readers * most,), -1, jnp.int32).at[position].set(...  8.24 us
    all_to_all x1, starting transfers between devices, per_device(): lax.all_to_all(mine, 'pb', split_axis=3, concat_axis=1, tiled=True)  7.97 us
  transfers between devices with their start and end apart: 2, of which 2 were waited for; matrix products, arithmetic and copies ran while one was open for 15% of the time, Pallas kernels for 0%

commit v1 on v0

--- a/solution.py
+++ b/solution.py
@@ -77,7 +77,9 @@
     my_vectors = r_elec[my_rows]
     keep = my_usable.astype(jnp.bfloat16)[:, None]
     span = q_local * width_sq
-    piece = lax.all_gather(rotated, "ka", axis=1, tiled=True)
+    piece = jnp.concatenate(
+        lax.all_to_all(jnp.stack([rotated] * lax.axis_size("ka")), "ka", 0, 0), axis=1
+    )
     count = piece.shape[1]
     cosine, sine = angle_tables(my_vectors, count, KGRID)
     left = jnp.concatenate([cosine * keep, sine * keep], axis=1)

time: 322 us -> 479 us (1.49)
  the two profiles are of different devices: /device:TPU:1 before, /device:TPU:135 now
where the time goes in v1:
time: 479 us; the launch traced here: 470 us
  waiting for transfers between devices  238 us (50%)
  local copies, waits for them, and re-layouts  112 us (23%)
  matrix products  72.7 us (15%)
  other arithmetic  25.2 us (5%)
  starting transfers between devices  21.5 us (4%)
    all_to_all x1, waiting for transfers between devices, per_device(): lax.all_to_all(jnp.stack([rotated] * lax.axis_size('ka')), 'ka', 0, 0)  238 us
    dot_general x1, matrix products, per_device(): summed = jnp.dot(left, right, preferred_element_type=jnp.float32)  64.3 us
    gather x1, local copies, waits for them, and re-layouts, slot_tables(): degen[source_row].astype(jnp.float32)  23 us
    slice x1, local copies, waits for them, and re-layouts, per_device(): z_imag = piece[:, :, 1].transpose(1, 0, 2).reshape(count, span)  23 us
    scatter x1, local copies, waits for them, and re-layouts, slot_tables(): source_row = jnp.full((readers * most,), -1, jnp.int32).at[position].set(...  20.2 us
    all_to_all x1, starting transfers between devices, per_device(): lax.all_to_all(jnp.stack([rotated] * lax.axis_size('ka')), 'ka', 0, 0)  11.3 us
    all_to_all x1, starting transfers between devices, per_device(): lax.all_to_all(mine, 'pb', split_axis=3, concat_axis=1, tiled=True)  10.2 us
    neg x1, other arithmetic, per_device(): lower = jnp.concatenate([z_imag, -z_real], axis=1)  9.64 us
  transfers between devices with their start and end apart: 2, of which 2 were waited for; matrix products, arithmetic and copies ran while one was open for 13% of the time, Pallas kernels for 0%

profile of v1, /device:TPU:135, one launch (start us, length us, event | category | flops | bytes accessed | tf_op | source)
XLA Modules:
  0.0 470.0 jit_solution(4981670677058924108)
XLA Ops:
  0.0 1.1 copy.73
  2.1 1.7 reshape.311
  4.3 1.5 fusion.24
  5.8 1.3 fusion.14
  7.9 2.0 reshape.277
  9.9 1.8 fusion.13
  14.2 1.5 stack.16
  17.3 7.6 %stack.19 = bf16[32,1,54,2,1600]{4,3,2,1,0:T(2,128)(2,1)} broadcast(bf16[54,2,1600]{2,1,0:T(2,128)(2,1)S(1)} %copy.78), dimensions={2,3,4} | broadcast | bytes 11404800 | tf_op jit(solution)/shard_map/stack | solution.py:81
  24.9 11.3 %all-to-all-start = ((bf16[32,1,54,2,1600]{4,3,2,1,0:T(2,128)(2,1)}), bf16[32,1,54,2,1600]{4,3,2,1,0:T(2,128)(2,1)}, u32[]{:S(2)}, u32[]{:S(2)}) async-start(bf16[32,1,54,2,1600]{4,3,2,1,0:T(2,128)(2,1)} %stack.19), calls=%async_computation | async-start | bytes 23003136 | tf_op jit(solution)/shard_map/all_to_all | solution.py:81
  36.2 9.1 %reduce-window.6 = s32[32,16,128]{2,1,0:T(8,128)S(1)} reduce-window(s32[32,16,128]{2,1,0:T(8,128)S(1)} %fusion.31, s32[]{:T(128)} %constant.88.clone.1), window={size=1x1x128 pad=0_0x0_0x127_0}, to_apply=%region_0.0 | reduce-window | flops 8323072 | bytes 524292 | tf_op jit(solution)/shard_map/reduce-window
  46.5 20.2 %scatter_custom_fusion = s32[4096]{0:T(1024)S(1)} fusion(s32[2048]{0:T(1024)S(1)} %bitcast.130, s32[2048]{0:T(1024)S(1)} %iota.45, s32[]{:T(128)} %constant.90.clone.1), kind=kCustom, calls=%fused_computation.92 | custom fusion | bytes 16388 | tf_op jit(solution)/shard_map/scatter | solution.py:36
  67.9 4.3 fusion.27
  72.2 237.8 %all-to-all-done = bf16[32,1,54,2,1600]{4,3,2,1,0:T(2,128)(2,1)} async-done(((bf16[32,1,54,2,1600]{4,3,2,1,0:T(2,128)(2,1)}), bf16[32,1,54,2,1600]{4,3,2,1,0:T(2,128)(2,1)}, u32[]{:S(2)}, u32[]{:S(2)}) %all-to-all-start) | async-done | bytes 11059232 | tf_op jit(solution)/shard_map/all_to_all | solution.py:81
  309.9 23.0 %fusion.65 = (bf16[1,1728,1,1600]{3,2,1,0:T(2,128)(2,1)}, bf16[1,1728,1,1600]{3,2,1,0:T(2,128)(2,1)}) fusion(bf16[1,1728,2,1600]{3,2,1,0:T(2,128)(2,1)} %bitcast.30), kind=kLoop, calls=%fused_computation.129 | loop fusion | bytes 22118400 | tf_op jit(solution)/shard_map/slice | solution.py:87
  332.9 9.6 %fusion.64 = (bf16[1728,1600]{1,0:T(8,128)(2,1)}, bf16[1728,1600]{1,0:T(8,128)(2,1)}) fusion(bf16[1,1728,1,1600]{3,2,1,0:T(2,128)(2,1)} %get-tuple-element.11), kind=kLoop, calls=%fused_computation.128 | loop fusion | flops 2764800 | bytes 16588800 | tf_op jit(solution)/shard_map/neg | solution.py:89
  342.6 5.2 %copy.111 = bf16[1,1728,1,1600]{3,1,2,0:T(8,128)(2,1)S(1)} copy(bf16[1,1728,1,1600]{3,2,1,0:T(2,128)(2,1)} %get-tuple-element.10) | data formatting | bytes 11059200
  347.7 64.3 %fusion.1 = f32[128,3200]{0,1:T(8,128)} fusion(bf16[1728,1600]{1,0:T(8,128)(2,1)} %get-tuple-element.8, bf16[1728,1600]{1,0:T(8,128)(2,1)S(1)} %bitcast.120, bf16[1728,1600]{1,0:T(8,128)(2,1)} %get-tuple-element.9, bf16[128,1728]{1,0:T(8,128)(2,1)S(1)} %get-tuple-element.17, bf16[128,1728]{1,0:T(8,128)(2,1)S(1)} %get-tuple-element.16), kind=kOutput, calls=%fused_computation.6 | convolution fusion | flops 2921398272 | bytes 19111936 | tf_op jit(solution)/shard_map/dot_general | solution.py:91
  412.1 1.5 slice_bitcast_fusion.1
  413.8 7.5 %copy.85 = bf16[128,1,2,1600]{0,2,1,3:T(2,128)(2,1)} copy(bf16[128,1,2,1600]{0,3,2,1:T(8,128)(2,1)S(1)} %fusion.6) | data formatting | bytes 1638400 | tf_op jit(solution)/shard_map/convert_element_type | solution.py:97
  421.3 10.2 %all-to-all-start.1 = ((bf16[128,1,2,1600]{0,2,1,3:T(2,128)(2,1)}), bf16[128,1,2,1600]{0,2,1,3:T(2,128)(2,1)S(1)}, u32[]{:S(2)}, u32[]{:S(2)}) async-start(bf16[128,1,2,1600]{0,2,1,3:T(2,128)(2,1)} %copy.85), calls=%async_computation.1 | async-start | bytes 1638400 | tf_op jit(solution)/shard_map/all_to_all | solution.py:98
  431.5 23.0 %gather_fusion.1 = s32[4096]{0:T(1024)S(1)} fusion(s32[2048]{0:T(1024)S(1)} %copy-done, s32[4096]{0:T(1024)S(1)} %get-tuple-element.18), kind=kCustom, calls=%fused_computation.1 | custom fusion | bytes 49152 | tf_op jit(solution)/shard_map/gather | solution.py:40
  455.8 2.0 reshape.282
  457.9 4.0 dot_general.47
  465.4 4.2 copy.90
  (59 shorter events, 13.5 us)
Async XLA Ops:
  0.0 431.5 %copy-start = (s32[2048]{0:T(1024)S(1)}, s32[2048]{0:T(1024)}, u32[]{:S(2)}) copy-start(s32[2048]{0:T(1024)} %param.11) | copy-start | bytes 24580
  0.0 2.1 copy-start.3
  5.8 1.3 copy-start.4
  9.9 1.8 copy-start.1
  12.7 3.1 copy-start.2
  24.9 11.3 %copy-start.5 = (s32[2048,1]{0,1:T(1,128)S(1)}, s32[2048,1]{0,1:T(1,128)}, u32[]{:S(2)}) copy-start(s32[2048,1]{0,1:T(1,128)} %param.12) | copy-start | bytes 24580
  24.9 285.0 %all-to-all-start = ((bf16[32,1,54,2,1600]{4,3,2,1,0:T(2,128)(2,1)}), bf16[32,1,54,2,1600]{4,3,2,1,0:T(2,128)(2,1)}, u32[]{:S(2)}, u32[]{:S(2)}) async-start(bf16[32,1,54,2,1600]{4,3,2,1,0:T(2,128)(2,1)} %stack.19), calls=%async_computation | async-start | bytes 23003136 | tf_op jit(solution)/shard_map/all_to_all | solution.py:81
  36.2 9.7 %copy-start.6 = (s32[2048,3]{0,1:T(4,128)S(1)}, s32[2048,3]{0,1:T(4,128)}, u32[]{:S(2)}) copy-start(s32[2048,3]{0,1:T(4,128)} %param.10) | copy-start | bytes 73732
  421.3 33.6 %all-to-all-start.1 = ((bf16[128,1,2,1600]{0,2,1,3:T(2,128)(2,1)}), bf16[128,1,2,1600]{0,2,1,3:T(2,128)(2,1)S(1)}, u32[]{:S(2)}, u32[]{:S(2)}) async-start(bf16[128,1,2,1600]{0,2,1,3:T(2,128)(2,1)} %copy.85), calls=%async_computation.1 | async-start | bytes 1638400 | tf_op jit(solution)/shard_map/all_to_all | solution.py:98
  431.5 23.2 %copy-start.7 = (s32[32,3]{0,1:T(4,128)S(1)}, s32[32,3]{0,1:T(4,128)}, u32[]{:S(2)}) copy-start(s32[32,3]{0,1:T(4,128)} %param.13) | copy-start | bytes 1156
